TPU v7x, 32 devices: a whole 2x2x4 slice. The times are simulated.
32 devices in a mesh: box: 8 (over z, x), path: 4 (over y, core).
Axes of the slice: x: 2, y: 2, z: 4, core: 2. Of those that a mesh axis runs over, the one named last changes fastest.
Arguments:
- features: float32 [1024, 9, 128], P('box'), may hold values from -6 to 6
- positions: float32 [3, 1024], P(None, 'box'), may hold values from 0 to 96, as said below
- cotangent: bfloat16 [1024, 9, 128], P('box'), may hold values from -6 to 6
- weights: float32 [8, 8, 128], P('path'), may hold values from -2 to 2
- neighbours: int32 [16, 3], P('box'), may hold values from 0 to 3, as said below
- send_list: int32 [8, 2], P('box'), may hold values from 0 to 1, as said below
Outputs:
- grad_features: float32 [1024, 9, 128], P(('box', 'path'))
- grad_weights: float32 [8, 8, 128], P('path')
Inputs may be any that keep to these rules, and one draw needn't show every extreme that they name: `positions`: stored block s of box b has a place g = b * 2 + (a permutation of 0 to 1 within the box) along a chain; its atoms lie near the points of a grid of spacing 1.5 with 4 x 4 points across and 4 along the third coordinate, the first coordinate between 6 g and 6 g + 6, each moved by at most 0.35 in each coordinate. Blocks whose places differ by two or more have no atoms within 5 of each other. `neighbours`: row g lists the block itself (its stored index), the block one place before it and the block one place after it along the chain, as table indices: below 2 the box's own stored blocks, 2 the block received from the previous box (its last block along the chain), 3 the block received from the next box (its first block along the chain). The relation is symmetric. send_list[b, 0] is the stored index of the first block of box b's stretch of the chain and send_list[b, 1] that of the last.
All inputs are finite; a program needn't handle non-finite values.
Results may differ from a plain program's by a relative error of at most 0.0045.
Values may be sent and summed in bfloat16 or wider, within the bound.
A program may use at most 64 MiB of HBM per device.

v0:
```python
import math
import jax
import jax.numpy as jnp
from jax import lax
from jax.sharding import PartitionSpec as P

BASIS = 8
BLOCK = 64
NEIGHBOURS = 3
PATHS = 8
cutoff_radius = 5.0
edge_scale = 0.2
basis_width = 0.8
root_three = math.sqrt(3.0)
path_terms = [
    [(0, [(0, 0, 1.0)])],
    [(0, [(1, 1, 1.0), (2, 2, 1.0), (3, 3, 1.0)])],
    [(1, [(1, 0, 1.0)]), (2, [(2, 0, 1.0)]), (3, [(3, 0, 1.0)])],
    [(1, [(0, 1, 1.0)]), (2, [(0, 2, 1.0)]), (3, [(0, 3, 1.0)])],
    [
        (4, [(4, 0, 1.0)]),
        (5, [(5, 0, 1.0)]),
        (6, [(6, 0, 1.0)]),
        (7, [(7, 0, 1.0)]),
        (8, [(8, 0, 1.0)]),
    ],
    [
        (4, [(0, 4, 1.0)]),
        (5, [(0, 5, 1.0)]),
        (6, [(0, 6, 1.0)]),
        (7, [(0, 7, 1.0)]),
        (8, [(0, 8, 1.0)]),
    ],
    [
        (1, [(3, 2, 1.0), (2, 3, -1.0)]),
        (2, [(1, 3, 1.0), (3, 1, -1.0)]),
        (3, [(2, 1, 1.0), (1, 2, -1.0)]),
    ],
    [(0, [(4, 4, 1.0), (5, 5, 1.0), (6, 6, 1.0), (7, 7, 1.0), (8, 8, 1.0)])],
]


def with_halo(cells, sides, width):
    for axis, dim in sides:
        count = lax.axis_size(axis)
        ends = count - 1
        head = lax.slice_in_dim(cells, 0, width, axis=dim)
        tail = lax.slice_in_dim(cells, cells.shape[dim] - width, cells.shape[dim], axis=dim)
        cells = jnp.concatenate(
            [
                lax.ppermute(tail, axis, [(i, (i + 1) % count) for i in range(ends)]),
                cells,
                lax.ppermute(head, axis, [((i + 1) % count, i) for i in range(ends)]),
            ],
            axis=dim,
        )
    return cells


def edge_tensor(anchor, target):
    offset = target[:, None, :] - anchor[:, :, None]
    square = jnp.sum(offset * offset, axis=0)
    inside = square > 0.01
    distance = jnp.sqrt(jnp.where(inside, square, 1.0))
    direction = offset / distance[None]
    envelope = jnp.where(
        inside & (distance < cutoff_radius),
        0.5 * (jnp.cos(math.pi * distance / cutoff_radius) + 1.0),
        0.0,
    )
    centres = (jnp.arange(BASIS, dtype=jnp.float32) + 0.5) * (cutoff_radius / BASIS)
    radial = (
        jnp.exp(-jnp.square((distance[None] - centres[:, None, None]) / basis_width))
        * (edge_scale * envelope)[None]
    )
    eastward = direction[0]
    northward = direction[1]
    upward = direction[2]
    harmonics = jnp.stack(
        [
            jnp.ones_like(eastward),
            eastward,
            northward,
            upward,
            root_three * eastward * northward,
            root_three * northward * upward,
            0.5 * (3.0 * upward * upward - 1.0),
            root_three * eastward * upward,
            0.5 * root_three * (eastward * eastward - northward * northward),
        ]
    )
    return (harmonics[:, None] * radial[None]).astype(jnp.bfloat16)


def forward_terms(paths, weights, edge_table, rounded):
    source_rows = rounded.shape[0]
    target_rows = edge_table.shape[2]
    channels = rounded.shape[2]
    outputs = [jnp.zeros((target_rows, channels), jnp.float32) for output in range(9)]
    for weight_slot, path_number in enumerate(paths):
        for output, term_list in path_terms[path_number]:
            pieces = []
            stacked = []
            for harmonic, source, factor in term_list:
                signed = edge_table[harmonic] if factor > 0 else -edge_table[harmonic]
                pieces.append(signed.reshape(BASIS * target_rows, source_rows))
                stacked.append(rounded[:, source, :])
            product = jnp.dot(
                jnp.concatenate(pieces, axis=1),
                jnp.concatenate(stacked, axis=0),
                preferred_element_type=jnp.float32,
            )
            product = product.reshape(BASIS, target_rows, channels)
            outputs[output] = outputs[output] + jnp.sum(
                weights[weight_slot][:, None, :] * product, axis=0
            )
    return jnp.stack(outputs, axis=1)


def transpose_terms(paths, weights, edge_table, cotangent_rows, source_features):
    rows = source_features.shape[0]
    channels = source_features.shape[2]
    outputs = [jnp.zeros((rows, channels), jnp.float32) for output in range(9)]
    weight_parts = []
    for weight_slot, path_number in enumerate(paths):
        weight_part = jnp.zeros((BASIS, channels), jnp.float32)
        for output, term_list in path_terms[path_number]:
            for harmonic, source, factor in term_list:
                gathered = lax.dot_general(
                    edge_table[harmonic],
                    cotangent_rows[:, output, :],
                    (((1,), (0,)), ((), ())),
                    preferred_element_type=jnp.float32,
                )
                outputs[source] = outputs[source] + factor * jnp.sum(
                    weights[weight_slot][:, None, :] * gathered, axis=0
                )
                weight_part = weight_part + factor * jnp.sum(
                    source_features[:, source, :][None] * gathered, axis=1
                )
        weight_parts.append(weight_part)
    return (jnp.stack(outputs, axis=1), jnp.stack(weight_parts, axis=0))


def gate_back(message, cotangent):
    incoming = cotangent.astype(jnp.float32)
    scalar = message[:, 0]
    sigma = jax.nn.sigmoid(scalar)
    slope = sigma * (1.0 + scalar * (1.0 - sigma))
    coupling = jnp.sum(incoming[:, 1:] * message[:, 1:], axis=1)
    leading = incoming[:, 0] * slope + sigma * (1.0 - sigma) * coupling
    others = incoming[:, 1:] * sigma[:, None]
    return jnp.concatenate([leading[:, None], others], axis=1).astype(jnp.bfloat16)


def on_device(features, positions, cotangent, weights, neighbours, send_list):
    local_blocks = neighbours.shape[0]
    local_rows = features.shape[0]
    channels = features.shape[2]
    block_features = features.reshape(local_blocks, BLOCK, 9, channels)
    block_places = positions.reshape(3, local_blocks, BLOCK).transpose(1, 0, 2)
    outgoing = send_list[0]
    padded_features, padded_places = (
        with_halo(block_features[outgoing], (("box", 0),), 1),
        with_halo(block_places[outgoing], (("box", 0),), 1),
    )
    table_features = jnp.concatenate(
        [block_features, padded_features[:1], padded_features[3:]], axis=0
    )
    table_places = jnp.concatenate([block_places, padded_places[:1], padded_places[3:]], axis=0)
    table_rounded = table_features.astype(jnp.bfloat16)
    group = lax.axis_index("path")
    share_rows = local_rows // lax.axis_size("path")
    cotangent_share = lax.dynamic_slice_in_dim(cotangent, group * share_rows, share_rows, 0)
    all_weights = lax.all_gather(weights, "path", axis=0, tiled=True)
    all_paths = list(range(PATHS))
    slab_rows = math.gcd(share_rows, BLOCK)
    slab_numbers = jnp.arange(share_rows // slab_rows, dtype=jnp.int32)

    def slab_anchor(slab_index):
        first_row = group * share_rows + slab_index * slab_rows
        block_number = first_row // BLOCK
        within_row = first_row % BLOCK
        anchor_rows = lax.dynamic_slice_in_dim(block_places[block_number], within_row, slab_rows, 1)
        return (block_number, within_row, anchor_rows)

    def forward_slab(slab_index):
        block_number, within_row, anchor_rows = slab_anchor(slab_index)
        total = jnp.zeros((slab_rows, 9, channels), jnp.float32)
        for neighbour in range(NEIGHBOURS):
            table_slot = neighbours[block_number, neighbour]
            edge_table = edge_tensor(anchor_rows, table_places[table_slot])
            total = total + forward_terms(
                all_paths, all_weights, edge_table, table_rounded[table_slot]
            )
        return total

    message_rows = lax.map(forward_slab, slab_numbers).reshape(share_rows, 9, channels)
    gate_rows = gate_back(message_rows, cotangent_share)
    message_cotangent = lax.all_gather(gate_rows, "path", axis=0, tiled=True)
    cotangent_blocks = message_cotangent.reshape(local_blocks, BLOCK, 9, channels)
    padded_gate = with_halo(cotangent_blocks[outgoing], (("box", 0),), 1)
    table_gate = jnp.concatenate([cotangent_blocks, padded_gate[:1], padded_gate[3:]], axis=0)

    def pull_slab(slab_index):
        block_number, within_row, anchor_rows = slab_anchor(slab_index)
        own_features = lax.dynamic_slice_in_dim(
            block_features[block_number], within_row, slab_rows, 0
        )
        total = jnp.zeros((slab_rows, 9, channels), jnp.float32)
        weight_total = jnp.zeros((PATHS, BASIS, channels), jnp.float32)
        for neighbour in range(NEIGHBOURS):
            table_slot = neighbours[block_number, neighbour]
            edge_table = edge_tensor(table_places[table_slot], anchor_rows)
            contribution, weight_part = transpose_terms(
                all_paths, all_weights, edge_table, table_gate[table_slot], own_features
            )
            total = total + contribution
            weight_total = weight_total + weight_part
        return (total, weight_total)

    totals, slab_weights = lax.map(pull_slab, slab_numbers)
    grad_features = totals.reshape(share_rows, 9, channels) + cotangent_share.astype(jnp.float32)
    weight_every = lax.psum(jnp.sum(slab_weights, axis=0), ("box", "path"))
    group_paths = PATHS // lax.axis_size("path")
    weight_total = lax.dynamic_slice_in_dim(weight_every, group * group_paths, group_paths, 0)
    return (grad_features, weight_total / math.sqrt(local_rows * lax.axis_size("box")))


def solution(mesh):
    placed = (
        P("box", None, None),
        P(None, "box"),
        P("box", None, None),
        P("path", None, None),
        P("box", None),
        P("box", None),
    )
    return jax.shard_map(
        on_device,
        mesh=mesh,
        in_specs=placed,
        out_specs=(P(("box", "path"), None, None), P("path", None, None)),
        check_vma=False,
    )
```

profile of v0, /device:TPU:0, one launch (start us, length us, event | category | flops | bytes accessed | tf_op | source)
XLA Modules:
  0.0 147.7 jit_solution(1303785314537078605)
XLA Ops:
  0.6 0.8 reshape.2374
  1.4 0.7 fusion.347
  2.1 0.6 gather_fusion
  2.6 4.9 %collective-permute-start = (f32[1,3,64]{2,1,0:T(4,128)S(1)}, f32[1,3,64]{2,1,0:T(4,128)S(1)}, u32[]{:S(2)}, u32[]{:S(2)}) collective-permute-start(f32[1,3,64]{2,1,0:T(4,128)S(1)} %get-tuple-element.590), channel_id=1, source_target_pairs={{0,4},{4,8},{8,12},{12,16},{16,20},{20,24},{24,28},{1,5},{5,9},{9,... | collective-permute-start | bytes 2312 | tf_op jit(solution)/shard_map/ppermute | solution.py:51
  7.5 1.3 collective-permute-start.1
  8.8 1.7 %gather_fusion.1 = bf16[2,64,9,128]{3,1,2,0:T(8,128)(2,1)S(1)} fusion(f32[2,64,9,128]{3,1,0,2:T(8,128)} %bitcast.899, s32[1024]{0:T(1024)S(1)} %pad_clamp_fusion), kind=kCustom, calls=%fused_computation.1 | custom fusion | bytes 589832 | tf_op jit(solution)/shard_map/gather | solution.py:164
  10.5 0.7 fusion.388
  11.3 5.2 %collective-permute-start.2 = (bf16[1,64,9,128]{3,1,2,0:T(8,128)(2,1)}, bf16[1,64,9,128]{3,1,2,0:T(8,128)(2,1)}, u32[]{:S(2)}, u32[]{:S(2)}) collective-permute-start(bf16[1,64,9,128]{3,1,2,0:T(8,128)(2,1)} %get-tuple-element.509), channel_id=1, source_target_pairs={{0,4},{4,8},{8,12},{12,16},{16,20},{20,24},{24,28},{1,5},{5,9},{9,... | collective-permute-start | bytes 442376 | tf_op jit(solution)/shard_map/ppermute | solution.py:51
  16.5 1.3 collective-permute-start.3
  18.0 0.7 constant_dynamic-slice_fusion.3
  20.0 5.2 %all_gather.6 = f32[8,8,128]{2,1,0:T(8,128)S(1)} all-gather(f32[2,8,128]{2,1,0:T(8,128)S(1)} %copy-done.55), channel_id=1, replica_groups=mesh['box'=8,'path'=4] {'path'}, dimensions={0}, use_global_device_ids=true | all-gather | bytes 40960 | tf_op jit(solution)/shard_map/all_gather | solution.py:175
  25.2 0.6 slice_bitcast_fusion.210
  25.8 0.7 slice_bitcast_fusion.96
  26.4 1.6 %dynamic-slice_convert_fusion = f32[32,9,128]{2,0,1:T(8,128)} fusion(bf16[128,9,128]{2,0,1:T(8,128)(2,1)} %param.8, s32[]{:T(128)S(6)} %select_n.212), kind=kLoop, calls=%fused_computation.489 | loop fusion | flops 36864 | bytes 221188 | tf_op jit(solution)/shard_map/convert_element_type | solution.py:146
  33.4 0.8 fusion.384
  34.3 0.7 fusion.385
  35.3 0.8 fusion.386
  36.1 0.7 bitcast_negate_fusion.7
  36.8 0.6 bitcast_negate_fusion.2
  37.4 0.6 bitcast_negate_fusion
  38.1 0.6 bitcast_negate_fusion.1
  38.7 0.7 bitcast_negate_fusion.3
  39.4 0.7 bitcast_negate_fusion.4
  40.0 0.6 bitcast_negate_fusion.8
  40.6 0.6 bitcast_negate_fusion.6
  42.0 0.5 copy-done.32
  42.8 0.8 copy-done.33
  43.7 1.8 %concatenate.157 = bf16[256,320]{1,0:T(8,128)(2,1)} concatenate(bf16[256,64]{1,0:T(8,128)(2,1)} %bitcast.946, bf16[256,64]{1,0:T(8,128)(2,1)} %bitcast.945, bf16[256,64]{1,0:T(8,128)(2,1)} %bitcast.944, bf16[256,64]{1,0:T(8,128)(2,1)} %bitcast.943, bf16[256,64]{1,0:T(8,128)(2,1)} %bitcast.942), dimensions={1} | concatenate | bytes 327680 | tf_op jit(solution)/shard_map/while/body/eval_jaxpr/concatenate | solution.py:109
  45.4 1.8 %concatenate.167 = bf16[256,320]{1,0:T(8,128)(2,1)} concatenate(bf16[256,64]{1,0:T(8,128)(2,1)} %bitcast.941, bf16[256,64]{1,0:T(8,128)(2,1)} %bitcast.940, bf16[256,64]{1,0:T(8,128)(2,1)} %bitcast.939, bf16[256,64]{1,0:T(8,128)(2,1)} %bitcast.938, bf16[256,64]{1,0:T(8,128)(2,1)} %bitcast.937), dimensions={1} | concatenate | bytes 327680 | tf_op jit(solution)/shard_map/while/body/eval_jaxpr/concatenate | solution.py:109
  47.2 1.8 %concatenate.147 = bf16[256,320]{1,0:T(8,128)(2,1)} concatenate(bf16[256,64]{1,0:T(8,128)(2,1)} %bitcast.936, bf16[256,64]{1,0:T(8,128)(2,1)} %bitcast.935, bf16[256,64]{1,0:T(8,128)(2,1)} %bitcast.934, bf16[256,64]{1,0:T(8,128)(2,1)} %bitcast.933, bf16[256,64]{1,0:T(8,128)(2,1)} %bitcast.932), dimensions={1} | concatenate | bytes 327680 | tf_op jit(solution)/shard_map/while/body/eval_jaxpr/concatenate | solution.py:109
  49.0 0.8 bitcast_negate_fusion.5
  49.8 1.1 pad_maximum_fusion
  51.1 0.9 copy-done.2
  60.0 0.2 fusion.102
  60.2 0.2 fusion.64
  60.9 0.2 fusion.94
  61.1 0.2 fusion.86
  61.4 0.2 fusion.58
  62.2 0.2 fusion.52
  62.6 0.2 fusion.78
  62.8 0.2 fusion.74
  63.8 0.3 copy-done.6
  64.9 0.7 copy-done.3
  65.7 6.0 %all_gather.7 = bf16[128,9,128]{2,0,1:T(8,128)(2,1)S(1)} all-gather(bf16[32,9,128]{2,0,1:T(8,128)(2,1)S(1)} %pad_maximum_fusion.1), channel_id=1, replica_groups=mesh['box'=8,'path'=4] {'path'}, dimensions={0}, use_global_device_ids=true | all-gather | bytes 368640 | tf_op jit(solution)/shard_map/all_gather | solution.py:200
  71.8 0.7 gather_fusion.2
  72.5 4.6 %collective-permute-start.4 = (bf16[1,64,9,128]{3,1,2,0:T(8,128)(2,1)S(1)}, bf16[1,64,9,128]{3,1,2,0:T(8,128)(2,1)S(1)}, u32[]{:S(2)}, u32[]{:S(2)}) collective-permute-start(bf16[1,64,9,128]{3,1,2,0:T(8,128)(2,1)S(1)} %get-tuple-element.508), channel_id=1, source_target_pairs={{0,4},{4,8},{8,12},{12,16},{16,20},{20,24},{24,28},{1,5},{5,9},{9,... | collective-permute-start | bytes 442376 | tf_op jit(solution)/shard_map/ppermute | solution.py:51
  77.1 1.5 collective-permute-start.5
  78.6 2.1 %collective-permute-done.4 = bf16[1,64,9,128]{3,1,2,0:T(8,128)(2,1)S(1)} collective-permute-done((bf16[1,64,9,128]{3,1,2,0:T(8,128)(2,1)S(1)}, bf16[1,64,9,128]{3,1,2,0:T(8,128)(2,1)S(1)}, u32[]{:S(2)}, u32[]{:S(2)}) %collective-permute-start.4) | collective-permute-done | bytes 147488 | tf_op jit(solution)/shard_map/ppermute | solution.py:51
  80.7 5.1 %collective-permute-done.5 = bf16[1,64,9,128]{3,1,2,0:T(8,128)(2,1)S(1)} collective-permute-done((bf16[1,64,9,128]{3,1,2,0:T(8,128)(2,1)S(1)}, bf16[1,64,9,128]{3,1,2,0:T(8,128)(2,1)S(1)}, u32[]{:S(2)}, u32[]{:S(2)}) %collective-permute-start.5) | collective-permute-done | bytes 147488 | tf_op jit(solution)/shard_map/ppermute | solution.py:53
  98.1 0.4 multiply_reduce_fusion.24
  98.5 0.2 copy-done.40
  98.8 0.4 multiply_reduce_fusion.8
  99.2 0.3 copy-done.47
  99.5 0.4 multiply_reduce_fusion.5
  99.9 0.3 copy-done.46
  100.2 0.4 multiply_reduce_fusion.6
  100.9 0.5 multiply_reduce_fusion.16
  101.8 0.2 copy-done.43
  102.1 0.3 multiply_reduce_fusion.1
  102.4 0.4 copy-done.41
  102.8 0.3 multiply_reduce_fusion
  103.4 41.7 %psum.7 = f32[8,8,128]{2,1,0:T(8,128)S(1)} all-reduce(f32[8,8,128]{2,1,0:T(8,128)S(1)} %add_add_fusion.2), channel_id=1, replica_groups=mesh['box'=8,'path'=4] {'box','path'}, use_global_device_ids=true, to_apply=%region_259.260 | all-reduce | flops 8192 | bytes 65536 | tf_op jit(solution)/shard_map/psum | solution.py:224
  145.1 0.6 dynamic-slice_multiply_fusion
  146.1 1.6 %add_add_fusion = f32[32,9,128]{2,0,1:T(8,128)} fusion(f32[32,9,128]{2,0,1:T(8,128)S(1)} %constant_dynamic-update-slice_fusion.104, f32[32,9,128]{2,0,1:T(8,128)S(1)} %constant_dynamic-update-slice_fusion.72, f32[32,9,128]{2,0,1:T(8,128)S(1)} %constant_dynamic-update-slice_fusion.88, bf16[128,9,128]{2,0,1:T(8,128)(2,1)} %param.8, s32[]{:T(128)S(6)} %select_n.212), kind=kLoop, calls=%fused_computation.252 | loop fusion | flops 147456 | bytes 663556 | tf_op jit(solution)/shard_map/add | solution.py:223
  (425 shorter events, 25.2 us)
Async XLA Ops:
  2.1 9.2 %copy-start.56 = (s32[1024]{0:T(1024)}, s32[1024]{0:T(1024)S(1)}, u32[]{:S(2)}) copy-start(s32[1024]{0:T(1024)S(1)} %pad_clamp_fusion) | copy-start | bytes 12292
  2.6 29.8 %collective-permute-start = (f32[1,3,64]{2,1,0:T(4,128)S(1)}, f32[1,3,64]{2,1,0:T(4,128)S(1)}, u32[]{:S(2)}, u32[]{:S(2)}) collective-permute-start(f32[1,3,64]{2,1,0:T(4,128)S(1)} %get-tuple-element.590), channel_id=1, source_target_pairs={{0,4},{4,8},{8,12},{12,16},{16,20},{20,24},{24,28},{1,5},{5,9},{9,... | collective-permute-start | bytes 2312 | tf_op jit(solution)/shard_map/ppermute | solution.py:51
  7.5 24.9 %collective-permute-start.1 = (f32[1,3,64]{2,1,0:T(4,128)S(1)}, f32[1,3,64]{2,1,0:T(4,128)S(1)}, u32[]{:S(2)}, u32[]{:S(2)}) collective-permute-start(f32[1,3,64]{2,1,0:T(4,128)S(1)} %get-tuple-element.591), channel_id=1, source_target_pairs={{4,0},{8,4},{12,8},{16,12},{20,16},{24,20},{28,24},{5,1},{9,5},{13... | collective-permute-start | bytes 2312 | tf_op jit(solution)/shard_map/ppermute | solution.py:53
  10.5 7.5 %copy-start = (f32[128,9,128]{2,0,1:T(8,128)S(1)}, f32[128,9,128]{2,0,1:T(8,128)}, u32[]{:S(2)}) copy-start(f32[128,9,128]{2,0,1:T(8,128)} %param.6) | copy-start | bytes 1769476
  10.5 7.5 %copy-start.57 = (s32[2,3]{1,0:T(2,128)S(1)}, s32[2,3]{1,0:T(2,128)}, u32[]{:S(2)}) copy-start(s32[2,3]{1,0:T(2,128)} %param.10) | copy-start | bytes 76
  10.5 9.5 %copy-start.55 = (f32[2,8,128]{2,1,0:T(8,128)S(1)}, f32[2,8,128]{2,1,0:T(8,128)}, u32[]{:S(2)}) copy-start(f32[2,8,128]{2,1,0:T(8,128)} %param.9) | copy-start | bytes 24580
  11.3 38.5 %collective-permute-start.2 = (bf16[1,64,9,128]{3,1,2,0:T(8,128)(2,1)}, bf16[1,64,9,128]{3,1,2,0:T(8,128)(2,1)}, u32[]{:S(2)}, u32[]{:S(2)}) collective-permute-start(bf16[1,64,9,128]{3,1,2,0:T(8,128)(2,1)} %get-tuple-element.509), channel_id=1, source_target_pairs={{0,4},{4,8},{8,12},{12,16},{16,20},{20,24},{24,28},{1,5},{5,9},{9,... | collective-permute-start | bytes 442376 | tf_op jit(solution)/shard_map/ppermute | solution.py:51
  16.5 33.4 %collective-permute-start.3 = (bf16[1,64,9,128]{3,1,2,0:T(8,128)(2,1)}, bf16[1,64,9,128]{3,1,2,0:T(8,128)(2,1)}, u32[]{:S(2)}, u32[]{:S(2)}) collective-permute-start(bf16[1,64,9,128]{3,1,2,0:T(8,128)(2,1)} %get-tuple-element.510), channel_id=1, source_target_pairs={{4,0},{8,4},{12,8},{16,12},{20,16},{24,20},{28,24},{5,1},{9,5},{13... | collective-permute-start | bytes 442376 | tf_op jit(solution)/shard_map/ppermute | solution.py:53
  34.1 2.0 %copy-start.9 = (bf16[1,8,32,64]{3,2,1,0:T(8,128)(2,1)}, bf16[1,8,32,64]{3,2,1,0:T(8,128)(2,1)S(1)}, u32[]{:S(2)}) copy-start(bf16[1,8,32,64]{3,2,1,0:T(8,128)(2,1)S(1)} %get-tuple-element.487) | copy-start | bytes 98308
  34.1 5.9 %copy-start.7 = (bf16[1,8,32,64]{3,2,1,0:T(8,128)(2,1)}, bf16[1,8,32,64]{3,2,1,0:T(8,128)(2,1)S(1)}, u32[]{:S(2)}) copy-start(bf16[1,8,32,64]{3,2,1,0:T(8,128)(2,1)S(1)} %get-tuple-element.480) | copy-start | bytes 98308
  34.1 6.5 %copy-start.11 = (bf16[1,8,32,64]{3,2,1,0:T(8,128)(2,1)}, bf16[1,8,32,64]{3,2,1,0:T(8,128)(2,1)S(1)}, u32[]{:S(2)}) copy-start(bf16[1,8,32,64]{3,2,1,0:T(8,128)(2,1)S(1)} %get-tuple-element.486) | copy-start | bytes 98308
  35.1 1.7 %copy-start.17 = (bf16[1,8,32,64]{3,2,1,0:T(8,128)(2,1)}, bf16[1,8,32,64]{3,2,1,0:T(8,128)(2,1)S(1)}, u32[]{:S(2)}) copy-start(bf16[1,8,32,64]{3,2,1,0:T(8,128)(2,1)S(1)} %get-tuple-element.488) | copy-start | bytes 98308
  35.1 2.3 %copy-start.15 = (bf16[1,8,32,64]{3,2,1,0:T(8,128)(2,1)}, bf16[1,8,32,64]{3,2,1,0:T(8,128)(2,1)S(1)}, u32[]{:S(2)}) copy-start(bf16[1,8,32,64]{3,2,1,0:T(8,128)(2,1)S(1)} %get-tuple-element.494) | copy-start | bytes 98308
  35.1 3.0 %copy-start.19 = (bf16[1,8,32,64]{3,2,1,0:T(8,128)(2,1)}, bf16[1,8,32,64]{3,2,1,0:T(8,128)(2,1)S(1)}, u32[]{:S(2)}) copy-start(bf16[1,8,32,64]{3,2,1,0:T(8,128)(2,1)S(1)} %get-tuple-element.495) | copy-start | bytes 98308
  35.3 1.5 %copy-start.1 = (bf16[9,8,32,64]{3,2,1,0:T(8,128)(2,1)}, bf16[9,8,32,64]{3,2,1,0:T(8,128)(2,1)S(1)}, u32[]{:S(2)}) copy-start(bf16[9,8,32,64]{3,2,1,0:T(8,128)(2,1)S(1)} %multiply_convert_fusion.3) | copy-start | bytes 884740
  36.1 5.4 %copy-start.13 = (bf16[1,8,32,64]{3,2,1,0:T(8,128)(2,1)}, bf16[1,8,32,64]{3,2,1,0:T(8,128)(2,1)S(1)}, u32[]{:S(2)}) copy-start(bf16[1,8,32,64]{3,2,1,0:T(8,128)(2,1)S(1)} %get-tuple-element.503) | copy-start | bytes 98308
  36.1 5.4 %copy-start.21 = (bf16[1,8,32,64]{3,2,1,0:T(8,128)(2,1)}, bf16[1,8,32,64]{3,2,1,0:T(8,128)(2,1)S(1)}, u32[]{:S(2)}) copy-start(bf16[1,8,32,64]{3,2,1,0:T(8,128)(2,1)S(1)} %get-tuple-element.502) | copy-start | bytes 98308
  41.9 0.7 copy-start.32
  42.6 0.9 copy-start.33
  50.9 1.1 copy-start.2
  50.9 1.1 copy-start.51
  50.9 1.3 copy-start.39
  51.0 1.9 %copy-start.49 = (f32[8,128]{1,0:T(8,128)S(1)}, f32[8,128]{1,0:T(8,128)}, u32[]{:S(2)}) copy-start(f32[8,128]{1,0:T(8,128)} %get-tuple-element.532) | copy-start | bytes 12292
  52.0 1.2 copy-start.37
  53.2 1.2 copy-start.53
  59.0 1.0 copy-start.20
  59.0 1.0 copy-start.31
  59.3 0.9 copy-start.16
  59.3 0.9 copy-start.18
  59.8 0.9 copy-start.30
  59.9 1.0 copy-start.29
  60.2 0.9 copy-start.23
  60.2 0.9 copy-start.28
  60.2 1.1 copy-start.14
  60.2 1.1 copy-start.22
  60.9 0.9 copy-start.27
  61.1 0.9 copy-start.12
  61.1 0.9 copy-start.25
  61.3 0.9 copy-start.8
  61.3 0.9 copy-start.10
  61.7 0.9 copy-start.26
  61.9 0.9 copy-start.24
  62.2 1.0 copy-start.4
  62.6 1.0 copy-start.5
  63.0 1.0 copy-start.6
  63.3 0.9 copy-start.36
  63.6 0.7 copy-start.34
  63.6 0.7 copy-start.35
  64.7 0.9 copy-start.3
  72.5 8.2 %collective-permute-start.4 = (bf16[1,64,9,128]{3,1,2,0:T(8,128)(2,1)S(1)}, bf16[1,64,9,128]{3,1,2,0:T(8,128)(2,1)S(1)}, u32[]{:S(2)}, u32[]{:S(2)}) collective-permute-start(bf16[1,64,9,128]{3,1,2,0:T(8,128)(2,1)S(1)} %get-tuple-element.508), channel_id=1, source_target_pairs={{0,4},{4,8},{8,12},{12,16},{16,20},{20,24},{24,28},{1,5},{5,9},{9,... | collective-permute-start | bytes 442376 | tf_op jit(solution)/shard_map/ppermute | solution.py:51
  77.1 8.7 %collective-permute-start.5 = (bf16[1,64,9,128]{3,1,2,0:T(8,128)(2,1)S(1)}, bf16[1,64,9,128]{3,1,2,0:T(8,128)(2,1)S(1)}, u32[]{:S(2)}, u32[]{:S(2)}) collective-permute-start(bf16[1,64,9,128]{3,1,2,0:T(8,128)(2,1)S(1)} %get-tuple-element.507), channel_id=1, source_target_pairs={{4,0},{8,4},{12,8},{16,12},{20,16},{24,20},{28,24},{5,1},{9,5},{13... | collective-permute-start | bytes 442376 | tf_op jit(solution)/shard_map/ppermute | solution.py:53
  97.1 0.9 copy-start.52
  97.2 0.9 copy-start.54
  98.0 0.7 copy-start.40
  98.1 0.7 copy-start.48
  98.8 0.7 copy-start.47
  99.5 0.7 copy-start.46
  100.2 0.7 copy-start.50
  100.9 0.7 copy-start.38
  100.9 0.7 copy-start.45
  101.4 0.7 copy-start.43
  101.4 0.7 copy-start.44
  102.1 0.7 copy-start.41
  102.1 0.7 copy-start.42
where the time goes:
time: 149 us; the launch traced here: 148 us
  blocking collectives  53 us (36%)
  matrix products  25 us (17%)
  local copies, waits for them, and re-layouts  20.3 us (14%)
  starting transfers between devices  18.7 us (13%)
  other arithmetic  14.5 us (10%)
  between operations  9.16 us (6%)
  waiting for transfers between devices  7.16 us (5%)
    psum x1, blocking collectives, on_device(): weight_every = lax.psum(jnp.sum(slab_weights, axis=0), ('box', 'path'))  41.7 us
    ppermute x3, starting transfers between devices, with_halo(): lax.ppermute(tail, axis, [(i, (i + 1) % count) for i in range(ends)])  14.6 us
    dot_general x93, matrix products, transpose_terms(): lax.dot_general(edge_table[harmonic], cotangent_rows[:, output, :], (((1,...  14.4 us
    dot_general x66, matrix products, forward_terms(): jnp.dot(jnp.concatenate(pieces, axis=1), jnp.concatenate(stacked, axis=0)...  10.6 us
    all_gather x1, blocking collectives, on_device(): message_cotangent = lax.all_gather(gate_rows, 'path', axis=0, tiled=True)  6.04 us
    unnamed x139, local copies, waits for them, and re-layouts  6.02 us
    neg x9, other arithmetic, forward_terms(): signed = edge_table[harmonic] if factor > 0 else -edge_table[harmonic]  6.01 us
    concatenate x3, local copies, waits for them, and re-layouts, forward_terms(): jnp.concatenate(pieces, axis=1)  5.3 us
  transfers between devices with their start and end apart: 6, of which 2 were waited for; matrix products, arithmetic and copies ran while one was open for 15% of the time, Pallas kernels for 0%

commit v1 on v0

--- a/solution.py
+++ b/solution.py
@@ -221,7 +221,13 @@
 
     totals, slab_weights = lax.map(pull_slab, slab_numbers)
     grad_features = totals.reshape(share_rows, 9, channels) + cotangent_share.astype(jnp.float32)
-    weight_every = lax.psum(jnp.sum(slab_weights, axis=0), ("box", "path"))
+
+    def turn_the_numbers(mine, mesh_dim, chip_axis="path"):
+        for w in (mesh_dim, chip_axis):
+            mine = lax.psum(mine, axis_name=w)
+        return mine
+
+    weight_every = turn_the_numbers(jnp.sum(slab_weights, axis=0), mesh_dim="box")
     group_paths = PATHS // lax.axis_size("path")
     weight_total = lax.dynamic_slice_in_dim(weight_every, group * group_paths, group_paths, 0)
     return (grad_features, weight_total / math.sqrt(local_rows * lax.axis_size("box")))

time: 149 us -> 154 us (1.034)
  blocking collectives: 53 us -> 58 us
    psum x1 -> x2, blocking collectives: 41.7 us -> 46.8 us  [turn_the_numbers(): mine = lax.psum(mine, axis_name=w)]
  transfers between devices with their start and end apart: 6 -> 6, of which waited for: 2 -> 2; matrix products, arithmetic and copies ran while one was open for 15% -> 14% of each run, Pallas kernels for 0% -> 0%
where the time goes in v1:
time: 154 us; the launch traced here: 153 us
  blocking collectives  58 us (38%)
  matrix products  25 us (16%)
  local copies, waits for them, and re-layouts  20.3 us (13%)
  starting transfers between devices  18.7 us (12%)
  other arithmetic  14.5 us (9%)
  between operations  9.16 us (6%)
  waiting for transfers between devices  7.16 us (5%)
    psum x2, blocking collectives, turn_the_numbers(): mine = lax.psum(mine, axis_name=w)  46.8 us
    ppermute x3, starting transfers between devices, with_halo(): lax.ppermute(tail, axis, [(i, (i + 1) % count) for i in range(ends)])  14.6 us
    dot_general x93, matrix products, transpose_terms(): lax.dot_general(edge_table[harmonic], cotangent_rows[:, output, :], (((1,...  14.4 us
    dot_general x66, matrix products, forward_terms(): jnp.dot(jnp.concatenate(pieces, axis=1), jnp.concatenate(stacked, axis=0)...  10.6 us
    all_gather x1, blocking collectives, on_device(): message_cotangent = lax.all_gather(gate_rows, 'path', axis=0, tiled=True)  6.04 us
    unnamed x139, local copies, waits for them, and re-layouts  6.02 us
    neg x9, other arithmetic, forward_terms(): signed = edge_table[harmonic] if factor > 0 else -edge_table[harmonic]  6.01 us
    concatenate x3, local copies, waits for them, and re-layouts, forward_terms(): jnp.concatenate(pieces, axis=1)  5.3 us
  transfers between devices with their start and end apart: 6, of which 2 were waited for; matrix products, arithmetic and copies ran while one was open for 14% of the time, Pallas kernels for 0%

profile of v1, /device:TPU:0, one launch (start us, length us, event | category | flops | bytes accessed | tf_op | source)
XLA Modules:
  0.0 152.8 jit_solution(3944988234929174868)
XLA Ops:
  0.6 0.8 reshape.2374
  1.4 0.7 fusion.347
  2.1 0.6 gather_fusion
  2.6 4.9 %collective-permute-start = (f32[1,3,64]{2,1,0:T(4,128)S(1)}, f32[1,3,64]{2,1,0:T(4,128)S(1)}, u32[]{:S(2)}, u32[]{:S(2)}) collective-permute-start(f32[1,3,64]{2,1,0:T(4,128)S(1)} %get-tuple-element.590), channel_id=1, source_target_pairs={{0,4},{4,8},{8,12},{12,16},{16,20},{20,24},{24,28},{1,5},{5,9},{9,... | collective-permute-start | bytes 2312 | tf_op jit(solution)/shard_map/ppermute | solution.py:51
  7.5 1.3 collective-permute-start.1
  8.8 1.7 %gather_fusion.1 = bf16[2,64,9,128]{3,1,2,0:T(8,128)(2,1)S(1)} fusion(f32[2,64,9,128]{3,1,0,2:T(8,128)} %bitcast.899, s32[1024]{0:T(1024)S(1)} %pad_clamp_fusion), kind=kCustom, calls=%fused_computation.1 | custom fusion | bytes 589832 | tf_op jit(solution)/shard_map/gather | solution.py:164
  10.5 0.7 fusion.388
  11.3 5.2 %collective-permute-start.2 = (bf16[1,64,9,128]{3,1,2,0:T(8,128)(2,1)}, bf16[1,64,9,128]{3,1,2,0:T(8,128)(2,1)}, u32[]{:S(2)}, u32[]{:S(2)}) collective-permute-start(bf16[1,64,9,128]{3,1,2,0:T(8,128)(2,1)} %get-tuple-element.509), channel_id=1, source_target_pairs={{0,4},{4,8},{8,12},{12,16},{16,20},{20,24},{24,28},{1,5},{5,9},{9,... | collective-permute-start | bytes 442376 | tf_op jit(solution)/shard_map/ppermute | solution.py:51
  16.5 1.3 collective-permute-start.3
  18.0 0.7 constant_dynamic-slice_fusion.3
  20.0 5.2 %all_gather.6 = f32[8,8,128]{2,1,0:T(8,128)S(1)} all-gather(f32[2,8,128]{2,1,0:T(8,128)S(1)} %copy-done.55), channel_id=1, replica_groups=mesh['box'=8,'path'=4] {'path'}, dimensions={0}, use_global_device_ids=true | all-gather | bytes 40960 | tf_op jit(solution)/shard_map/all_gather | solution.py:175
  25.2 0.6 slice_bitcast_fusion.210
  25.8 0.7 slice_bitcast_fusion.96
  26.4 1.6 %dynamic-slice_convert_fusion = f32[32,9,128]{2,0,1:T(8,128)} fusion(bf16[128,9,128]{2,0,1:T(8,128)(2,1)} %param.8, s32[]{:T(128)S(6)} %select_n.212), kind=kLoop, calls=%fused_computation.489 | loop fusion | flops 36864 | bytes 221188 | tf_op jit(solution)/shard_map/convert_element_type | solution.py:146
  33.4 0.8 fusion.384
  34.3 0.7 fusion.385
  35.3 0.8 fusion.386
  36.1 0.7 bitcast_negate_fusion.7
  36.8 0.6 bitcast_negate_fusion.2
  37.4 0.6 bitcast_negate_fusion
  38.1 0.6 bitcast_negate_fusion.1
  38.7 0.7 bitcast_negate_fusion.3
  39.4 0.7 bitcast_negate_fusion.4
  40.0 0.6 bitcast_negate_fusion.8
  40.6 0.6 bitcast_negate_fusion.6
  42.0 0.5 copy-done.32
  42.8 0.8 copy-done.33
  43.7 1.8 %concatenate.157 = bf16[256,320]{1,0:T(8,128)(2,1)} concatenate(bf16[256,64]{1,0:T(8,128)(2,1)} %bitcast.946, bf16[256,64]{1,0:T(8,128)(2,1)} %bitcast.945, bf16[256,64]{1,0:T(8,128)(2,1)} %bitcast.944, bf16[256,64]{1,0:T(8,128)(2,1)} %bitcast.943, bf16[256,64]{1,0:T(8,128)(2,1)} %bitcast.942), dimensions={1} | concatenate | bytes 327680 | tf_op jit(solution)/shard_map/while/body/eval_jaxpr/concatenate | solution.py:109
  45.4 1.8 %concatenate.167 = bf16[256,320]{1,0:T(8,128)(2,1)} concatenate(bf16[256,64]{1,0:T(8,128)(2,1)} %bitcast.941, bf16[256,64]{1,0:T(8,128)(2,1)} %bitcast.940, bf16[256,64]{1,0:T(8,128)(2,1)} %bitcast.939, bf16[256,64]{1,0:T(8,128)(2,1)} %bitcast.938, bf16[256,64]{1,0:T(8,128)(2,1)} %bitcast.937), dimensions={1} | concatenate | bytes 327680 | tf_op jit(solution)/shard_map/while/body/eval_jaxpr/concatenate | solution.py:109
  47.2 1.8 %concatenate.147 = bf16[256,320]{1,0:T(8,128)(2,1)} concatenate(bf16[256,64]{1,0:T(8,128)(2,1)} %bitcast.936, bf16[256,64]{1,0:T(8,128)(2,1)} %bitcast.935, bf16[256,64]{1,0:T(8,128)(2,1)} %bitcast.934, bf16[256,64]{1,0:T(8,128)(2,1)} %bitcast.933, bf16[256,64]{1,0:T(8,128)(2,1)} %bitcast.932), dimensions={1} | concatenate | bytes 327680 | tf_op jit(solution)/shard_map/while/body/eval_jaxpr/concatenate | solution.py:109
  49.0 0.8 bitcast_negate_fusion.5
  49.8 1.1 pad_maximum_fusion
  51.1 0.9 copy-done.2
  60.0 0.2 fusion.102
  60.2 0.2 fusion.64
  60.9 0.2 fusion.94
  61.1 0.2 fusion.86
  61.4 0.2 fusion.58
  62.2 0.2 fusion.52
  62.8 0.2 fusion.74
  63.8 0.3 copy-done.6
  64.9 0.7 copy-done.3
  65.7 6.0 %all_gather.7 = bf16[128,9,128]{2,0,1:T(8,128)(2,1)S(1)} all-gather(bf16[32,9,128]{2,0,1:T(8,128)(2,1)S(1)} %pad_maximum_fusion.1), channel_id=1, replica_groups=mesh['box'=8,'path'=4] {'path'}, dimensions={0}, use_global_device_ids=true | all-gather | bytes 368640 | tf_op jit(solution)/shard_map/all_gather | solution.py:200
  71.8 0.7 gather_fusion.2
  72.5 4.6 %collective-permute-start.4 = (bf16[1,64,9,128]{3,1,2,0:T(8,128)(2,1)S(1)}, bf16[1,64,9,128]{3,1,2,0:T(8,128)(2,1)S(1)}, u32[]{:S(2)}, u32[]{:S(2)}) collective-permute-start(bf16[1,64,9,128]{3,1,2,0:T(8,128)(2,1)S(1)} %get-tuple-element.508), channel_id=1, source_target_pairs={{0,4},{4,8},{8,12},{12,16},{16,20},{20,24},{24,28},{1,5},{5,9},{9,... | collective-permute-start | bytes 442376 | tf_op jit(solution)/shard_map/ppermute | solution.py:51
  77.1 1.5 collective-permute-start.5
  78.6 2.1 %collective-permute-done.4 = bf16[1,64,9,128]{3,1,2,0:T(8,128)(2,1)S(1)} collective-permute-done((bf16[1,64,9,128]{3,1,2,0:T(8,128)(2,1)S(1)}, bf16[1,64,9,128]{3,1,2,0:T(8,128)(2,1)S(1)}, u32[]{:S(2)}, u32[]{:S(2)}) %collective-permute-start.4) | collective-permute-done | bytes 147488 | tf_op jit(solution)/shard_map/ppermute | solution.py:51
  80.7 5.1 %collective-permute-done.5 = bf16[1,64,9,128]{3,1,2,0:T(8,128)(2,1)S(1)} collective-permute-done((bf16[1,64,9,128]{3,1,2,0:T(8,128)(2,1)S(1)}, bf16[1,64,9,128]{3,1,2,0:T(8,128)(2,1)S(1)}, u32[]{:S(2)}, u32[]{:S(2)}) %collective-permute-start.5) | collective-permute-done | bytes 147488 | tf_op jit(solution)/shard_map/ppermute | solution.py:53
  98.1 0.4 multiply_reduce_fusion.24
  98.5 0.2 copy-done.40
  98.8 0.4 multiply_reduce_fusion.8
  99.2 0.3 copy-done.47
  99.5 0.4 multiply_reduce_fusion.5
  99.9 0.3 copy-done.46
  100.2 0.4 multiply_reduce_fusion.6
  100.9 0.5 multiply_reduce_fusion.16
  101.8 0.2 copy-done.43
  102.1 0.3 multiply_reduce_fusion.1
  102.4 0.4 copy-done.41
  102.8 0.3 multiply_reduce_fusion
  103.4 36.6 %psum.14 = f32[8,8,128]{2,1,0:T(8,128)S(1)} all-reduce(f32[8,8,128]{2,1,0:T(8,128)S(1)} %add_add_fusion.2), channel_id=1, replica_groups=mesh['box'=8,'path'=4] {'box'}, use_global_device_ids=true, to_apply=%region_259.260 | all-reduce | flops 8192 | bytes 65536 | tf_op jit(solution)/shard_map/psum | solution.py:227
  139.9 10.3 %psum.15 = f32[8,8,128]{2,1,0:T(8,128)S(1)} all-reduce(f32[8,8,128]{2,1,0:T(8,128)S(1)} %psum.14), channel_id=1, replica_groups=mesh['box'=8,'path'=4] {'path'}, use_global_device_ids=true, to_apply=%region_260.261 | all-reduce | flops 8192 | bytes 65536 | tf_op jit(solution)/shard_map/psum | solution.py:227
  150.2 0.6 dynamic-slice_multiply_fusion
  151.2 1.6 %add_add_fusion = f32[32,9,128]{2,0,1:T(8,128)} fusion(f32[32,9,128]{2,0,1:T(8,128)S(1)} %constant_dynamic-update-slice_fusion.104, f32[32,9,128]{2,0,1:T(8,128)S(1)} %constant_dynamic-update-slice_fusion.72, f32[32,9,128]{2,0,1:T(8,128)S(1)} %constant_dynamic-update-slice_fusion.88, bf16[128,9,128]{2,0,1:T(8,128)(2,1)} %param.8, s32[]{:T(128)S(6)} %select_n.212), kind=kLoop, calls=%fused_computation.252 | loop fusion | flops 147456 | bytes 663556 | tf_op jit(solution)/shard_map/add | solution.py:223
  (426 shorter events, 25.4 us)
Async XLA Ops:
  2.1 9.2 %copy-start.56 = (s32[1024]{0:T(1024)}, s32[1024]{0:T(1024)S(1)}, u32[]{:S(2)}) copy-start(s32[1024]{0:T(1024)S(1)} %pad_clamp_fusion) | copy-start | bytes 12292
  2.6 29.8 %collective-permute-start = (f32[1,3,64]{2,1,0:T(4,128)S(1)}, f32[1,3,64]{2,1,0:T(4,128)S(1)}, u32[]{:S(2)}, u32[]{:S(2)}) collective-permute-start(f32[1,3,64]{2,1,0:T(4,128)S(1)} %get-tuple-element.590), channel_id=1, source_target_pairs={{0,4},{4,8},{8,12},{12,16},{16,20},{20,24},{24,28},{1,5},{5,9},{9,... | collective-permute-start | bytes 2312 | tf_op jit(solution)/shard_map/ppermute | solution.py:51
  7.5 24.9 %collective-permute-start.1 = (f32[1,3,64]{2,1,0:T(4,128)S(1)}, f32[1,3,64]{2,1,0:T(4,128)S(1)}, u32[]{:S(2)}, u32[]{:S(2)}) collective-permute-start(f32[1,3,64]{2,1,0:T(4,128)S(1)} %get-tuple-element.591), channel_id=1, source_target_pairs={{4,0},{8,4},{12,8},{16,12},{20,16},{24,20},{28,24},{5,1},{9,5},{13... | collective-permute-start | bytes 2312 | tf_op jit(solution)/shard_map/ppermute | solution.py:53
  10.5 7.5 %copy-start = (f32[128,9,128]{2,0,1:T(8,128)S(1)}, f32[128,9,128]{2,0,1:T(8,128)}, u32[]{:S(2)}) copy-start(f32[128,9,128]{2,0,1:T(8,128)} %param.6) | copy-start | bytes 1769476
  10.5 7.5 %copy-start.57 = (s32[2,3]{1,0:T(2,128)S(1)}, s32[2,3]{1,0:T(2,128)}, u32[]{:S(2)}) copy-start(s32[2,3]{1,0:T(2,128)} %param.10) | copy-start | bytes 76
  10.5 9.5 %copy-start.55 = (f32[2,8,128]{2,1,0:T(8,128)S(1)}, f32[2,8,128]{2,1,0:T(8,128)}, u32[]{:S(2)}) copy-start(f32[2,8,128]{2,1,0:T(8,128)} %param.9) | copy-start | bytes 24580
  11.3 38.5 %collective-permute-start.2 = (bf16[1,64,9,128]{3,1,2,0:T(8,128)(2,1)}, bf16[1,64,9,128]{3,1,2,0:T(8,128)(2,1)}, u32[]{:S(2)}, u32[]{:S(2)}) collective-permute-start(bf16[1,64,9,128]{3,1,2,0:T(8,128)(2,1)} %get-tuple-element.509), channel_id=1, source_target_pairs={{0,4},{4,8},{8,12},{12,16},{16,20},{20,24},{24,28},{1,5},{5,9},{9,... | collective-permute-start | bytes 442376 | tf_op jit(solution)/shard_map/ppermute | solution.py:51
  16.5 33.4 %collective-permute-start.3 = (bf16[1,64,9,128]{3,1,2,0:T(8,128)(2,1)}, bf16[1,64,9,128]{3,1,2,0:T(8,128)(2,1)}, u32[]{:S(2)}, u32[]{:S(2)}) collective-permute-start(bf16[1,64,9,128]{3,1,2,0:T(8,128)(2,1)} %get-tuple-element.510), channel_id=1, source_target_pairs={{4,0},{8,4},{12,8},{16,12},{20,16},{24,20},{28,24},{5,1},{9,5},{13... | collective-permute-start | bytes 442376 | tf_op jit(solution)/shard_map/ppermute | solution.py:53
  34.1 2.0 %copy-start.9 = (bf16[1,8,32,64]{3,2,1,0:T(8,128)(2,1)}, bf16[1,8,32,64]{3,2,1,0:T(8,128)(2,1)S(1)}, u32[]{:S(2)}) copy-start(bf16[1,8,32,64]{3,2,1,0:T(8,128)(2,1)S(1)} %get-tuple-element.487) | copy-start | bytes 98308
  34.1 5.9 %copy-start.7 = (bf16[1,8,32,64]{3,2,1,0:T(8,128)(2,1)}, bf16[1,8,32,64]{3,2,1,0:T(8,128)(2,1)S(1)}, u32[]{:S(2)}) copy-start(bf16[1,8,32,64]{3,2,1,0:T(8,128)(2,1)S(1)} %get-tuple-element.480) | copy-start | bytes 98308
  34.1 6.5 %copy-start.11 = (bf16[1,8,32,64]{3,2,1,0:T(8,128)(2,1)}, bf16[1,8,32,64]{3,2,1,0:T(8,128)(2,1)S(1)}, u32[]{:S(2)}) copy-start(bf16[1,8,32,64]{3,2,1,0:T(8,128)(2,1)S(1)} %get-tuple-element.486) | copy-start | bytes 98308
  35.1 1.7 %copy-start.17 = (bf16[1,8,32,64]{3,2,1,0:T(8,128)(2,1)}, bf16[1,8,32,64]{3,2,1,0:T(8,128)(2,1)S(1)}, u32[]{:S(2)}) copy-start(bf16[1,8,32,64]{3,2,1,0:T(8,128)(2,1)S(1)} %get-tuple-element.488) | copy-start | bytes 98308
  35.1 2.3 %copy-start.15 = (bf16[1,8,32,64]{3,2,1,0:T(8,128)(2,1)}, bf16[1,8,32,64]{3,2,1,0:T(8,128)(2,1)S(1)}, u32[]{:S(2)}) copy-start(bf16[1,8,32,64]{3,2,1,0:T(8,128)(2,1)S(1)} %get-tuple-element.494) | copy-start | bytes 98308
  35.1 3.0 %copy-start.19 = (bf16[1,8,32,64]{3,2,1,0:T(8,128)(2,1)}, bf16[1,8,32,64]{3,2,1,0:T(8,128)(2,1)S(1)}, u32[]{:S(2)}) copy-start(bf16[1,8,32,64]{3,2,1,0:T(8,128)(2,1)S(1)} %get-tuple-element.495) | copy-start | bytes 98308
  35.3 1.5 copy-start.1
  36.1 5.4 %copy-start.13 = (bf16[1,8,32,64]{3,2,1,0:T(8,128)(2,1)}, bf16[1,8,32,64]{3,2,1,0:T(8,128)(2,1)S(1)}, u32[]{:S(2)}) copy-start(bf16[1,8,32,64]{3,2,1,0:T(8,128)(2,1)S(1)} %get-tuple-element.503) | copy-start | bytes 98308
  36.1 5.4 %copy-start.21 = (bf16[1,8,32,64]{3,2,1,0:T(8,128)(2,1)}, bf16[1,8,32,64]{3,2,1,0:T(8,128)(2,1)S(1)}, u32[]{:S(2)}) copy-start(bf16[1,8,32,64]{3,2,1,0:T(8,128)(2,1)S(1)} %get-tuple-element.502) | copy-start | bytes 98308
  41.9 0.7 copy-start.32
  42.6 0.9 copy-start.33
  50.9 1.1 copy-start.2
  50.9 1.1 copy-start.51
  50.9 1.3 copy-start.39
  51.0 1.9 %copy-start.49 = (f32[8,128]{1,0:T(8,128)S(1)}, f32[8,128]{1,0:T(8,128)}, u32[]{:S(2)}) copy-start(f32[8,128]{1,0:T(8,128)} %get-tuple-element.532) | copy-start | bytes 12292
  52.0 1.2 copy-start.37
  53.2 1.2 copy-start.53
  59.0 1.0 copy-start.20
  59.0 1.0 copy-start.31
  59.3 0.9 copy-start.16
  59.3 0.9 copy-start.18
  59.8 0.9 copy-start.30
  59.9 1.0 copy-start.29
  60.2 0.9 copy-start.23
  60.2 0.9 copy-start.28
  60.2 1.1 copy-start.14
  60.2 1.1 copy-start.22
  60.9 0.9 copy-start.27
  61.1 0.9 copy-start.12
  61.1 0.9 copy-start.25
  61.3 0.9 copy-start.8
  61.3 0.9 copy-start.10
  61.7 0.9 copy-start.26
  61.9 0.9 copy-start.24
  62.2 1.0 copy-start.4
  62.6 1.0 copy-start.5
  63.0 1.0 copy-start.6
  63.3 0.9 copy-start.36
  63.6 0.7 copy-start.34
  63.6 0.7 copy-start.35
  64.7 0.9 copy-start.3
  72.5 8.2 %collective-permute-start.4 = (bf16[1,64,9,128]{3,1,2,0:T(8,128)(2,1)S(1)}, bf16[1,64,9,128]{3,1,2,0:T(8,128)(2,1)S(1)}, u32[]{:S(2)}, u32[]{:S(2)}) collective-permute-start(bf16[1,64,9,128]{3,1,2,0:T(8,128)(2,1)S(1)} %get-tuple-element.508), channel_id=1, source_target_pairs={{0,4},{4,8},{8,12},{12,16},{16,20},{20,24},{24,28},{1,5},{5,9},{9,... | collective-permute-start | bytes 442376 | tf_op jit(solution)/shard_map/ppermute | solution.py:51
  77.1 8.7 %collective-permute-start.5 = (bf16[1,64,9,128]{3,1,2,0:T(8,128)(2,1)S(1)}, bf16[1,64,9,128]{3,1,2,0:T(8,128)(2,1)S(1)}, u32[]{:S(2)}, u32[]{:S(2)}) collective-permute-start(bf16[1,64,9,128]{3,1,2,0:T(8,128)(2,1)S(1)} %get-tuple-element.507), channel_id=1, source_target_pairs={{4,0},{8,4},{12,8},{16,12},{20,16},{24,20},{28,24},{5,1},{9,5},{13... | collective-permute-start | bytes 442376 | tf_op jit(solution)/shard_map/ppermute | solution.py:53
  97.1 0.9 copy-start.52
  97.2 0.9 copy-start.54
  98.0 0.7 copy-start.40
  98.1 0.7 copy-start.48
  98.8 0.7 copy-start.47
  99.5 0.7 copy-start.46
  100.2 0.7 copy-start.50
  100.9 0.7 copy-start.38
  100.9 0.7 copy-start.45
  101.4 0.7 copy-start.43
  101.4 0.7 copy-start.44
  102.1 0.7 copy-start.41
  102.1 0.7 copy-start.42
